TPU v7x, 32 devices: a whole 2x2x4 slice. The times are simulated.
32 devices in a mesh: grp: 2 (over y), tm: 4 (over z), space: 2 (over x), obs: 2 (over core).
Axes of the slice: x: 2, y: 2, z: 4, core: 2. Of those that a mesh axis runs over, the one named last changes fastest.
Arguments:
- obs_panel: bfloat16 [8192, 768], P(('grp', 'tm', 'space', 'obs')), parts along dimension 0, may hold values from -0.375 to 0.375
- node_index: int32 [8192], P(('grp', 'tm', 'space', 'obs')), parts along dimension 0, may hold values from 0 to 767
- weight: bfloat16 [8192], P(('grp', 'tm', 'space', 'obs')), parts along dimension 0, may hold values from 0.049804688 to 0.5
- residual: bfloat16 [8192], P(('grp', 'tm', 'space', 'obs')), parts along dimension 0, may hold values from -6 to 6
- route_time: int32 [8192], P(('grp', 'tm', 'space', 'obs')), parts along dimension 0, may hold values from 0 to 3, as said below
- spatial_prec: float32 [8, 768, 768], P(('grp', 'tm'), ('space', 'obs')), parts along dimension 0, as said below
- ar_coef: float32 [8], P(('grp', 'tm')), parts along dimension 0, may hold values from 0.5 to 0.85
- prior_rhs: float32 [8, 768], P(('grp', 'tm'), ('space', 'obs')), parts along dimension 0, may hold values from -6 to 6
Outputs:
- reduced_diag: float32 [8, 768, 768], P(('grp', 'tm'), ('space', 'obs')), parts along dimension 0
- fill_block: float32 [8, 768, 768], P(('grp', 'tm'), ('space', 'obs')), parts along dimension 0
- reduced_rhs: float32 [8, 768], P(('grp', 'tm'), ('space', 'obs')), parts along dimension 0
There are 2 independent parts, one for each index of `grp`. A program takes and returns all parts, laid end to end along the dimension named above; each array names one. Nothing has to cross between parts.
Inputs may be any that keep to these rules, and one draw needn't show every extreme that they name: `route_time`: each device's 256 rows name each time block at most 128 times; in every draw one time block receives exactly 128 rows from every device's block of rows. `spatial_prec`: each block is symmetric positive definite.
All inputs are finite; a program needn't handle non-finite values.
Results may differ from a plain program's by a relative error of at most 0.0044.
Values may be sent and summed in bfloat16 or wider, within the bound.
No kernel may reach another device: no remote copies, remote signals or barrier semaphores. Data moves between devices by JAX's collectives and lax.ppermute only.
A program may use at most 64 MiB of HBM per device.

v0:
```python
import jax
import jax.numpy as jnp
from jax import lax
from jax.sharding import PartitionSpec as P


def from_behind(value, axis, steps):
    count = lax.axis_size(axis)
    pairs = [(source, (source + steps) % count) for source in range(count)]
    return lax.ppermute(value, axis, pairs)


def slot_table(route_time, n_times, capacity):
    marks = (route_time[:, None] == lax.iota(jnp.int32, n_times)[None, :]).astype(jnp.int32)
    before = jnp.cumsum(marks, axis=0) - marks
    rank = jnp.sum(before * marks, axis=1)
    return route_time * capacity + rank


def row_products(left_rows, right_rows):
    return lax.dot_general(
        left_rows, right_rows, (((1,), (1,)), ((), ())), preferred_element_type=jnp.float32
    )


def to_time(payload, shift_by):
    return from_behind(payload, "tm", shift_by)


def eliminate(diag_rows, rhs_rows, left_cols, right_cols, with_turn):
    shard_rows = diag_rows.shape[0]
    full_diag, full_rhs = (
        lax.all_gather(diag_rows, ("space", "obs"), axis=0, tiled=True),
        lax.all_gather(rhs_rows, ("space", "obs"), axis=0, tiled=True),
    )
    factor = jnp.linalg.cholesky(full_diag)
    stacked = jnp.concatenate([left_cols, right_cols, full_rhs[:, None]], axis=1)
    solved = lax.linalg.triangular_solve(factor, stacked, left_side=True, lower=True)
    left_y = solved[:, :shard_rows]
    right_y = solved[:, shard_rows : 2 * shard_rows]
    reduced = solved[:, 2 * shard_rows]
    up_left = jnp.dot(reduced, left_y, precision=lax.Precision.HIGHEST)
    up_right = jnp.dot(reduced, right_y, precision=lax.Precision.HIGHEST)
    left_rows = left_y.T.astype(jnp.bfloat16)
    right_rows = right_y.T.astype(jnp.bfloat16)
    piece_left, piece_right = lax.all_gather(
        (left_rows, right_rows), ("space", "obs"), axis=0, tiled=True
    )
    results = (
        row_products(left_rows, piece_left),
        row_products(right_rows, piece_right),
        -row_products(left_rows, piece_right),
    )
    if with_turn:
        results = results + (-row_products(right_rows, piece_left),)
    turned = None
    if with_turn:
        turned = results[3]
    return (results[0], results[1], results[2], turned, up_left, up_right)


def local(obs_panel, node_index, weight, residual, route_time, spatial_prec, ar_coef, prior_rhs):
    n_times = lax.axis_size("tm")
    time_index = lax.axis_index("tm")
    cell_index = lax.axis_index(("space", "obs"))
    rows_dev, node_count = obs_panel.shape
    shard_rows = spatial_prec.shape[1]
    capacity = 2 * rows_dev // n_times
    slot_count = n_times * capacity
    weighted_res = (weight.astype(jnp.float32) * residual.astype(jnp.float32)).astype(jnp.bfloat16)
    node_hits = (node_index[:, None] == lax.iota(jnp.int32, node_count)[None, :]).astype(
        jnp.float32
    )
    design = (obs_panel.astype(jnp.float32) + node_hits).astype(jnp.bfloat16)
    slot_index = slot_table(route_time, n_times, capacity)
    send_design = jnp.zeros((slot_count, node_count), jnp.bfloat16).at[slot_index].set(design)
    send_weight = jnp.zeros((slot_count,), jnp.bfloat16).at[slot_index].set(weight)
    send_res = jnp.zeros((slot_count,), jnp.bfloat16).at[slot_index].set(weighted_res)
    arrived = (
        lax.all_to_all(
            send_design.reshape(n_times, capacity, node_count),
            "tm",
            split_axis=0,
            concat_axis=0,
            tiled=True,
        ),
        lax.all_to_all(
            send_weight.reshape(n_times, capacity), "tm", split_axis=0, concat_axis=0, tiled=True
        ),
        lax.all_to_all(
            send_res.reshape(n_times, capacity), "tm", split_axis=0, concat_axis=0, tiled=True
        ),
    )
    slot_design = arrived[0].reshape(slot_count, node_count)
    slot_weight = arrived[1].reshape(slot_count)
    slot_res = arrived[2].reshape(slot_count)
    weighted = (slot_weight.astype(jnp.float32)[:, None] * slot_design.astype(jnp.float32)).astype(
        jnp.bfloat16
    )
    grad_part = jnp.dot(slot_res, slot_design, preferred_element_type=jnp.float32)
    gram_part = lax.psum_scatter(
        lax.dot_general(
            slot_design, weighted, (((0,), (0,)), ((), ())), preferred_element_type=jnp.float32
        ),
        ("space", "obs"),
        scatter_dimension=0,
        tiled=True,
    )
    grad_full = lax.psum(grad_part, ("space", "obs"))
    grad_mine = lax.dynamic_slice_in_dim(grad_full, cell_index * shard_rows, shard_rows)
    own_prec = spatial_prec[0]
    own_coef = ar_coef[0]
    next_prec, next_coef_arr = to_time((own_prec, ar_coef), -1)
    next_coef = next_coef_arr[0]
    diag_one = own_prec + next_coef * next_coef * next_prec + gram_part
    rhs_one = prior_rhs[0] + grad_mine
    left_cols = (-own_coef * own_prec).T
    right_cols = (-next_coef * next_prec).T
    loss_left, loss_right, fill_one, turn_one, up_left, up_right = eliminate(
        diag_one, rhs_one, left_cols, right_cols, True
    )
    from_right = to_time((loss_left, up_left, turn_one), -1)
    from_left = to_time((loss_right, up_right, fill_one), 1)
    even_time = time_index % 2 == 0
    diag_two = jnp.where(even_time, diag_one - from_right[0] - from_left[0], diag_one)
    rhs_two = jnp.where(even_time, rhs_one - from_right[1] - from_left[1], rhs_one)
    loss_left2, loss_right2, fill_two, unused_turn, up_left2, up_right2 = eliminate(
        diag_two, rhs_two, from_left[2].T, from_right[2].T, False
    )
    back_right = to_time((loss_left2, up_left2), -2)
    back_left = to_time((loss_right2, up_right2), 2)
    survive = time_index % 4 == 0
    diag_three = jnp.where(survive, diag_two - back_right[0] - back_left[0], diag_two)
    rhs_three = jnp.where(survive, rhs_two - back_right[1] - back_left[1], rhs_two)
    fill_out = jnp.where(
        time_index % 2 == 1,
        fill_one,
        jnp.where(time_index % 4 == 2, fill_two, jnp.zeros_like(fill_two)),
    )
    return (diag_three[None], fill_out[None], rhs_three[None])


def solution(mesh):
    return jax.shard_map(
        local,
        mesh=mesh,
        in_specs=(
            P(("grp", "tm", "space", "obs"), None),
            P(("grp", "tm", "space", "obs")),
            P(("grp", "tm", "space", "obs")),
            P(("grp", "tm", "space", "obs")),
            P(("grp", "tm", "space", "obs")),
            P(("grp", "tm"), ("space", "obs"), None),
            P(("grp", "tm")),
            P(("grp", "tm"), ("space", "obs")),
        ),
        out_specs=(
            P(("grp", "tm"), ("space", "obs"), None),
            P(("grp", "tm"), ("space", "obs"), None),
            P(("grp", "tm"), ("space", "obs")),
        ),
        check_vma=False,
    )
```

profile of v0, /device:TPU:0, one launch (start us, length us, event | category | flops | bytes accessed | tf_op | source)
XLA Modules:
  0.0 761.7 jit_solution(14472734522458335414)
XLA Ops:
  13.7 6.3 all-to-all-start.1
  25.6 3.5 all-to-all-start
  29.1 19.2 %all-to-all-done = bf16[4,128,768]{1,2,0:T(8,128)(2,1)S(1)} async-done(((bf16[4,128,768]{1,2,0:T(8,128)(2,1)}), bf16[4,128,768]{1,2,0:T(8,128)(2,1)S(1)}, u32[]{:S(2)}, u32[]{:S(2)}) %all-to-all-start) | async-done | bytes 786464 | tf_op jit(solution)/shard_map/all_to_all | solution.py:80
  53.0 12.3 %collective-permute-done = f32[1]{0:T(128)} collective-permute-done((f32[1]{0:T(128)}, f32[1]{0:T(128)}, u32[]{:S(2)}, u32[]{:S(2)}) %collective-permute-start) | collective-permute-done | bytes 36 | tf_op jit(solution)/shard_map/ppermute | solution.py:10
  67.1 15.5 %reduce-scatter.4.cloned.1.call-done = f32[192,768]{1,0:T(8,128)} async-done(((f32[768,768]{1,0:T(8,128)}), f32[192,768]{1,0:T(8,128)}) %reduce-scatter.4.cloned.1.call-update) | async-done | bytes 589840 | tf_op jit(solution)/shard_map/reduce_scatter | solution.py:101
  87.5 4.6 all-to-all-start.2
  93.4 4.2 all-to-all-done.2
  98.0 6.5 psum.7
  104.7 5.9 all-reduce.1
  111.7 3.4 copy.53
  118.6 11.7 %cholesky.453 = f32[128,128]{1,0:T(8,128)S(1)} custom-call(f32[128,128]{1,0:T(8,128)S(1)} %cholesky.669), custom_call_target="Cholesky" | custom-call | tf_op jit(solution)/shard_map/jit(cholesky)/cholesky | solution.py:36
  130.3 9.8 %custom-call.41 = f32[1,128,128]{1,2,0:T(8,128)S(1)} custom-call(f32[1,128,128]{2,1,0:T(8,128)S(1)} %get-tuple-element.107), custom_call_target="InvertDiagBlocksLowerTriangular" | custom-call | tf_op jit(solution)/shard_map/jit(cholesky)/cholesky | solution.py:36
  143.1 11.7 %cholesky.472 = f32[128,128]{1,0:T(8,128)S(1)} custom-call(f32[128,128]{1,0:T(8,128)S(1)} %cholesky.673), custom_call_target="Cholesky" | custom-call | tf_op jit(solution)/shard_map/jit(cholesky)/cholesky | solution.py:36
  154.8 10.3 %custom-call.42 = f32[1,128,128]{1,2,0:T(8,128)S(1)} custom-call(f32[1,128,128]{2,1,0:T(8,128)S(1)} %get-tuple-element.104), custom_call_target="InvertDiagBlocksLowerTriangular" | custom-call | tf_op jit(solution)/shard_map/jit(cholesky)/cholesky | solution.py:36
  167.1 11.7 %cholesky.493 = f32[128,128]{1,0:T(8,128)S(1)} custom-call(f32[128,128]{1,0:T(8,128)S(1)} %cholesky.678), custom_call_target="Cholesky" | custom-call | tf_op jit(solution)/shard_map/jit(cholesky)/cholesky | solution.py:36
  179.4 9.8 %custom-call.43 = f32[1,128,128]{1,2,0:T(8,128)S(1)} custom-call(f32[1,128,128]{2,1,0:T(8,128)S(1)} %get-tuple-element.101), custom_call_target="InvertDiagBlocksLowerTriangular" | custom-call | tf_op jit(solution)/shard_map/jit(cholesky)/cholesky | solution.py:36
  191.1 11.9 %cholesky.512 = f32[128,128]{1,0:T(8,128)S(1)} custom-call(f32[128,128]{1,0:T(8,128)S(1)} %cholesky.683), custom_call_target="Cholesky" | custom-call | tf_op jit(solution)/shard_map/jit(cholesky)/cholesky | solution.py:36
  203.7 9.8 %custom-call.44 = f32[1,128,128]{1,2,0:T(8,128)S(1)} custom-call(f32[1,128,128]{2,1,0:T(8,128)S(1)} %get-tuple-element.98), custom_call_target="InvertDiagBlocksLowerTriangular" | custom-call | tf_op jit(solution)/shard_map/jit(cholesky)/cholesky | solution.py:36
  215.3 11.7 %cholesky.531 = f32[128,128]{1,0:T(8,128)S(1)} custom-call(f32[128,128]{1,0:T(8,128)S(1)} %cholesky.688), custom_call_target="Cholesky" | custom-call | tf_op jit(solution)/shard_map/jit(cholesky)/cholesky | solution.py:36
  227.8 9.8 %custom-call.45 = f32[1,128,128]{1,2,0:T(8,128)S(1)} custom-call(f32[1,128,128]{2,1,0:T(8,128)S(1)} %get-tuple-element.95), custom_call_target="InvertDiagBlocksLowerTriangular" | custom-call | tf_op jit(solution)/shard_map/jit(cholesky)/cholesky | solution.py:36
  239.1 12.1 %cholesky.548 = f32[128,128]{1,0:T(8,128)S(1)} custom-call(f32[128,128]{1,0:T(8,128)S(1)} %convolution_subtract_fusion.4), custom_call_target="Cholesky" | custom-call | tf_op jit(solution)/shard_map/jit(cholesky)/cholesky | solution.py:36
  258.0 16.9 %while.4 = (s32[]{:T(128)}, f32[768,768]{1,0:T(8,128)}, s32[6,2]{0,1:T(2,128)S(1)}, f32[6,128,128]{2,1,0:T(8,128)S(1)}, s32[]{:T(128)}) while((s32[]{:T(128)}, f32[768,768]{1,0:T(8,128)}, s32[6,2]{0,1:T(2,128)S(1)}, f32[6,128,128]{2,1,0:T(8,128)S(1)}, s32[]{:T(128)}) %tuple.88), condition=%wide.while_cond, body=%wide.while_body.sunk | while | flops 2 | bytes 131189 | solution.py:38
  274.8 59.0 %custom-call.46 = f32[6,128,128]{1,2,0:T(8,128)S(1)} custom-call(f32[6,128,128]{2,1,0:T(8,128)S(1)} %get-tuple-element.19), custom_call_target="InvertDiagBlocksLowerTriangular" | custom-call | tf_op jit(solution)/shard_map/triangular_solve/custom-call.5 | solution.py:38
  347.5 14.8 %all-gather.9.cloned.1.call-done = bf16[768,768]{1,0:T(8,128)(2,1)} async-done(((bf16[192,768]{1,0:T(8,128)(2,1)}), bf16[768,768]{1,0:T(8,128)(2,1)}) %all-gather.9.cloned.1.call-update) | async-done | bytes 1179664 | tf_op jit(solution)/shard_map/all_gather | solution.py:46
  364.9 3.3 collective-permute-start.2
  368.3 12.9 %all-gather.11.cloned.1.call-done = bf16[768,768]{1,0:T(8,128)(2,1)} async-done(((bf16[192,768]{1,0:T(8,128)(2,1)}), bf16[768,768]{1,0:T(8,128)(2,1)}) %all-gather.11.cloned.1.call-update) | async-done | bytes 1179664 | tf_op jit(solution)/shard_map/all_gather | solution.py:46
  385.3 16.1 %collective-permute-done.3 = f32[192,768]{1,0:T(8,128)} collective-permute-done((f32[192,768]{1,0:T(8,128)}, f32[192,768]{1,0:T(8,128)}, u32[]{:S(2)}, u32[]{:S(2)}) %collective-permute-start.3) | collective-permute-done | bytes 589856 | tf_op jit(solution)/shard_map/ppermute | solution.py:10
  408.2 3.3 collective-permute-start.6
  412.1 19.5 %collective-permute-done.6 = f32[192]{0:T(256)S(1)} collective-permute-done((f32[192]{0:T(256)S(1)}, f32[192]{0:T(256)S(1)}, u32[]{:S(2)}, u32[]{:S(2)}) %collective-permute-start.6) | collective-permute-done | bytes 800 | tf_op jit(solution)/shard_map/ppermute | solution.py:10
  432.8 5.9 all-reduce.2
  439.9 3.3 copy.55
  446.6 11.7 %cholesky.563 = f32[128,128]{1,0:T(8,128)S(1)} custom-call(f32[128,128]{1,0:T(8,128)S(1)} %cholesky.692), custom_call_target="Cholesky" | custom-call | tf_op jit(solution)/shard_map/jit(cholesky)/cholesky | solution.py:36
  459.0 9.8 %custom-call.47 = f32[1,128,128]{1,2,0:T(8,128)S(1)} custom-call(f32[1,128,128]{2,1,0:T(8,128)S(1)} %get-tuple-element.91), custom_call_target="InvertDiagBlocksLowerTriangular" | custom-call | tf_op jit(solution)/shard_map/jit(cholesky)/cholesky | solution.py:36
  471.8 11.7 %cholesky.582 = f32[128,128]{1,0:T(8,128)S(1)} custom-call(f32[128,128]{1,0:T(8,128)S(1)} %cholesky.696), custom_call_target="Cholesky" | custom-call | tf_op jit(solution)/shard_map/jit(cholesky)/cholesky | solution.py:36
  484.1 10.0 %custom-call.48 = f32[1,128,128]{1,2,0:T(8,128)S(1)} custom-call(f32[1,128,128]{2,1,0:T(8,128)S(1)} %get-tuple-element.88), custom_call_target="InvertDiagBlocksLowerTriangular" | custom-call | tf_op jit(solution)/shard_map/jit(cholesky)/cholesky | solution.py:36
  496.1 11.7 %cholesky.603 = f32[128,128]{1,0:T(8,128)S(1)} custom-call(f32[128,128]{1,0:T(8,128)S(1)} %cholesky.701), custom_call_target="Cholesky" | custom-call | tf_op jit(solution)/shard_map/jit(cholesky)/cholesky | solution.py:36
  508.4 9.8 %custom-call.49 = f32[1,128,128]{1,2,0:T(8,128)S(1)} custom-call(f32[1,128,128]{2,1,0:T(8,128)S(1)} %get-tuple-element.85), custom_call_target="InvertDiagBlocksLowerTriangular" | custom-call | tf_op jit(solution)/shard_map/jit(cholesky)/cholesky | solution.py:36
  520.1 12.1 %cholesky.622 = f32[128,128]{1,0:T(8,128)S(1)} custom-call(f32[128,128]{1,0:T(8,128)S(1)} %cholesky.706), custom_call_target="Cholesky" | custom-call | tf_op jit(solution)/shard_map/jit(cholesky)/cholesky | solution.py:36
  532.9 9.8 %custom-call.50 = f32[1,128,128]{1,2,0:T(8,128)S(1)} custom-call(f32[1,128,128]{2,1,0:T(8,128)S(1)} %get-tuple-element.82), custom_call_target="InvertDiagBlocksLowerTriangular" | custom-call | tf_op jit(solution)/shard_map/jit(cholesky)/cholesky | solution.py:36
  544.5 11.7 %cholesky.641 = f32[128,128]{1,0:T(8,128)S(1)} custom-call(f32[128,128]{1,0:T(8,128)S(1)} %cholesky.711), custom_call_target="Cholesky" | custom-call | tf_op jit(solution)/shard_map/jit(cholesky)/cholesky | solution.py:36
  557.0 9.8 %custom-call.51 = f32[1,128,128]{1,2,0:T(8,128)S(1)} custom-call(f32[1,128,128]{2,1,0:T(8,128)S(1)} %get-tuple-element.79), custom_call_target="InvertDiagBlocksLowerTriangular" | custom-call | tf_op jit(solution)/shard_map/jit(cholesky)/cholesky | solution.py:36
  568.3 11.9 %cholesky.658 = f32[128,128]{1,0:T(8,128)S(1)} custom-call(f32[128,128]{1,0:T(8,128)S(1)} %slice_subtract_fusion.24), custom_call_target="Cholesky" | custom-call | tf_op jit(solution)/shard_map/jit(cholesky)/cholesky | solution.py:36
  586.2 17.4 %while.5 = (s32[]{:T(128)}, f32[768,768]{1,0:T(8,128)}, s32[6,2]{0,1:T(2,128)S(1)}, f32[6,128,128]{2,1,0:T(8,128)S(1)}, s32[]{:T(128)}) while((s32[]{:T(128)}, f32[768,768]{1,0:T(8,128)}, s32[6,2]{0,1:T(2,128)S(1)}, f32[6,128,128]{2,1,0:T(8,128)S(1)}, s32[]{:T(128)}) %tuple.108), condition=%wide.while_cond.clone, body=%wide.while_body.clone.sunk | while | flops 2 | bytes 131189 | solution.py:38
  603.6 59.0 %custom-call.52 = f32[6,128,128]{1,2,0:T(8,128)S(1)} custom-call(f32[6,128,128]{2,1,0:T(8,128)S(1)} %get-tuple-element.20), custom_call_target="InvertDiagBlocksLowerTriangular" | custom-call | tf_op jit(solution)/shard_map/triangular_solve/custom-call.5 | solution.py:38
  678.6 14.6 %all-gather.17.cloned.1.call-done = bf16[768,768]{1,0:T(8,128)(2,1)} async-done(((bf16[192,768]{1,0:T(8,128)(2,1)}), bf16[768,768]{1,0:T(8,128)(2,1)}) %all-gather.17.cloned.1.call-update) | async-done | bytes 1179664 | tf_op jit(solution)/shard_map/all_gather | solution.py:46
  693.1 2.7 fusion.107
  698.3 14.5 %all-gather.15.cloned.1.call-done = bf16[768,768]{1,0:T(8,128)(2,1)} async-done(((bf16[192,768]{1,0:T(8,128)(2,1)}), bf16[768,768]{1,0:T(8,128)(2,1)}) %all-gather.15.cloned.1.call-update) | async-done | bytes 1179664 | tf_op jit(solution)/shard_map/all_gather | solution.py:46
  718.9 31.6 %collective-permute-done.10 = f32[192]{0:T(256)S(1)} collective-permute-done((f32[192]{0:T(256)S(1)}, f32[192]{0:T(256)S(1)}, u32[]{:S(2)}, u32[]{:S(2)}) %collective-permute-start.10) | collective-permute-done | bytes 800 | tf_op jit(solution)/shard_map/ppermute | solution.py:10
  (235 shorter events, 153.2 us)
Async XLA Ops:
  13.7 11.8 %all-to-all-start.1 = ((bf16[4,1,128]{2,1,0:T(2,128)(2,1)}), bf16[4,1,128]{2,1,0:T(2,128)(2,1)S(1)}, u32[]{:S(2)}, u32[]{:S(2)}) async-start(bf16[4,1,128]{2,1,0:T(2,128)(2,1)} %copy.49), calls=%async_computation.1 | async-start | bytes 4096 | tf_op jit(solution)/shard_map/all_to_all | solution.py:87
  25.6 22.8 %all-to-all-start = ((bf16[4,128,768]{1,2,0:T(8,128)(2,1)}), bf16[4,128,768]{1,2,0:T(8,128)(2,1)S(1)}, u32[]{:S(2)}, u32[]{:S(2)}) async-start(bf16[4,128,768]{1,2,0:T(8,128)(2,1)} %copy.48), calls=%async_computation | async-start | bytes 1572864 | tf_op jit(solution)/shard_map/all_to_all | solution.py:80
  29.1 53.6 %reduce-scatter.4.cloned.1.call-start = ((), (), s32[]{:S(2)}) async-start(), calls=%async_computation.10 | async-start | bytes 2949120 | tf_op jit(solution)/shard_map/reduce_scatter | solution.py:101
  48.3 2.3 copy-start.12
  50.6 34.1 %copy-start.14 = (bf16[256]{0:T(256)(128)(2,1)S(1)}, bf16[256]{0:T(256)(128)(2,1)}, u32[]{:S(2)}) copy-start(bf16[256]{0:T(256)(128)(2,1)} %param.13) | copy-start | bytes 1540
  50.6 34.1 %copy-start.15 = (bf16[256]{0:T(256)(128)(2,1)S(1)}, bf16[256]{0:T(256)(128)(2,1)}, u32[]{:S(2)}) copy-start(bf16[256]{0:T(256)(128)(2,1)} %param.14) | copy-start | bytes 1540
  50.6 41.5 %copy-start.16 = (u32[32]{0:T(128)S(1)}, u32[32]{0:T(128)}, u32[]{:S(2)}) copy-start(u32[32]{0:T(128)} %constant.230) | copy-start | bytes 388
  50.6 61.1 %all-gather.7.cloned.1.call-start = ((), (), s32[]{:S(2)}) async-start(), calls=%async_computation.4 | async-start | bytes 2949120 | tf_op jit(solution)/shard_map/all_gather | solution.py:33
  50.7 16.4 %collective-permute-start.1 = (f32[192,768]{1,0:T(8,128)S(1)}, f32[192,768]{1,0:T(8,128)S(1)}, u32[]{:S(2)}, u32[]{:S(2)}) collective-permute-start(f32[192,768]{1,0:T(8,128)S(1)} %bitcast.221), channel_id=1, source_target_pairs={{0,12},{4,0},{8,4},{12,8},{1,13},{5,1},{9,5},{13,9},{2,14},{6,2},{... | collective-permute-start | bytes 1769480 | tf_op jit(solution)/shard_map/ppermute | solution.py:10
  52.2 13.0 %collective-permute-start = (f32[1]{0:T(128)}, f32[1]{0:T(128)}, u32[]{:S(2)}, u32[]{:S(2)}) collective-permute-start(f32[1]{0:T(128)} %param.17), channel_id=1, source_target_pairs={{0,12},{4,0},{8,4},{12,8},{1,13},{5,1},{9,5},{13,9},{2,14},{6,2},{... | collective-permute-start | bytes 20 | tf_op jit(solution)/shard_map/ppermute | solution.py:10
  82.7 21.8 %copy-start.13 = (f32[1,192]{1,0:T(1,128)S(1)}, f32[1,192]{1,0:T(1,128)}, u32[]{:S(2)}) copy-start(f32[1,192]{1,0:T(1,128)} %param.18) | copy-start | bytes 2308
  87.5 10.1 %all-to-all-start.2 = ((bf16[4,1,128]{2,1,0:T(2,128)(2,1)}), bf16[4,1,128]{2,1,0:T(2,128)(2,1)S(1)}, u32[]{:S(2)}, u32[]{:S(2)}) async-start(bf16[4,1,128]{2,1,0:T(2,128)(2,1)} %copy.54), calls=%async_computation.2 | async-start | bytes 4096 | tf_op jit(solution)/shard_map/all_to_all | solution.py:90
  92.1 270.2 %all-gather.9.cloned.1.call-start = ((), (), s32[]{:S(2)}) async-start(), calls=%async_computation.5 | async-start | bytes 1474560 | tf_op jit(solution)/shard_map/all_gather | solution.py:46
  111.7 3.5 copy-start
  117.1 1.4 copy-start.3
  257.9 78.6 %copy-start.6 = (f32[768,385]{0,1:T(8,128)S(1)}, f32[768,385]{0,1:T(8,128)}, u32[]{:S(2)}) copy-start(f32[768,385]{0,1:T(8,128)} %pad_maximum_fusion) | copy-start | bytes 3548164
  346.8 34.4 %all-gather.11.cloned.1.call-start = ((), (), s32[]{:S(2)}) async-start(), calls=%async_computation.6 | async-start | bytes 1474560 | tf_op jit(solution)/shard_map/all_gather | solution.py:46
  347.4 54.0 %copy-start.5 = (f32[192,768]{1,0:T(8,128)S(1)}, f32[192,768]{1,0:T(8,128)}, u32[]{:S(2)}) copy-start(f32[192,768]{1,0:T(8,128)} %get-tuple-element.54) | copy-start | bytes 1769476
  347.4 92.4 %all-gather.13.cloned.1.call-start = ((), (), s32[]{:S(2)}) async-start(), calls=%async_computation.7 | async-start | bytes 2949120 | tf_op jit(solution)/shard_map/all_gather | solution.py:33
  364.9 38.7 %copy-start.8 = (bf16[768,768]{1,0:T(8,128)(2,1)S(1)}, bf16[768,768]{1,0:T(8,128)(2,1)}, u32[]{:S(2)}) copy-start(bf16[768,768]{1,0:T(8,128)(2,1)} %all-gather.9.cloned.1.call-done) | copy-start | bytes 3538948
  364.9 20.4 %collective-permute-start.2 = (f32[192,768]{1,0:T(8,128)}, f32[192,768]{1,0:T(8,128)}, u32[]{:S(2)}, u32[]{:S(2)}) collective-permute-start(f32[192,768]{1,0:T(8,128)} %fusion.149), channel_id=1, source_target_pairs={{0,12},{4,0},{8,4},{12,8},{1,13},{5,1},{9,5},{13,9},{2,14},{6,2},{... | collective-permute-start | bytes 1769480 | tf_op jit(solution)/shard_map/ppermute | solution.py:10
  383.8 17.6 %collective-permute-start.3 = (f32[192,768]{1,0:T(8,128)}, f32[192,768]{1,0:T(8,128)}, u32[]{:S(2)}, u32[]{:S(2)}) collective-permute-start(f32[192,768]{1,0:T(8,128)} %fusion.151), channel_id=1, source_target_pairs={{0,4},{4,8},{8,12},{12,0},{1,5},{5,9},{9,13},{13,1},{2,6},{6,10},{... | collective-permute-start | bytes 1769480 | tf_op jit(solution)/shard_map/ppermute | solution.py:10
  403.6 289.5 %all-gather.17.cloned.1.call-start = ((), (), s32[]{:S(2)}) async-start(), calls=%async_computation.9 | async-start | bytes 1474560 | tf_op jit(solution)/shard_map/all_gather | solution.py:46
  403.7 2.9 copy-start.10
  405.0 33.7 %collective-permute-start.5 = (f32[192,768]{1,0:T(8,128)}, f32[192,768]{1,0:T(8,128)S(1)}, u32[]{:S(2)}, u32[]{:S(2)}) collective-permute-start(f32[192,768]{1,0:T(8,128)} %convolution_negate_fusion.1), channel_id=1, source_target_pairs={{0,12},{4,0},{8,4},{12,8},{1,13},{5,1},{9,5},{13,9},{2,14},{6,2},{... | collective-permute-start | bytes 1769480 | tf_op jit(solution)/shard_map/ppermute | solution.py:10
  407.1 32.7 %copy-start.11 = (f32[192,768]{1,0:T(8,128)}, f32[192,768]{1,0:T(8,128)S(1)}, u32[]{:S(2)}) copy-start(f32[192,768]{1,0:T(8,128)S(1)} %convolution_negate_fusion.2) | copy-start | bytes 1769476
  407.1 31.6 %collective-permute-start.4 = (f32[192,768]{1,0:T(8,128)S(1)}, f32[192,768]{1,0:T(8,128)S(1)}, u32[]{:S(2)}, u32[]{:S(2)}) collective-permute-start(f32[192,768]{1,0:T(8,128)S(1)} %convolution_negate_fusion.2), channel_id=1, source_target_pairs={{0,4},{4,8},{8,12},{12,0},{1,5},{5,9},{9,13},{13,1},{2,6},{6,10},{... | collective-permute-start | bytes 1769480 | tf_op jit(solution)/shard_map/ppermute | solution.py:10
  408.2 23.4 %collective-permute-start.6 = (f32[192]{0:T(256)S(1)}, f32[192]{0:T(256)S(1)}, u32[]{:S(2)}, u32[]{:S(2)}) collective-permute-start(f32[192]{0:T(256)S(1)} %bitcast.229), channel_id=1, source_target_pairs={{0,12},{4,0},{8,4},{12,8},{1,13},{5,1},{9,5},{13,9},{2,14},{6,2},{... | collective-permute-start | bytes 2312 | tf_op jit(solution)/shard_map/ppermute | solution.py:10
  412.1 20.5 %collective-permute-start.7 = (f32[192]{0:T(256)S(1)}, f32[192]{0:T(256)S(1)}, u32[]{:S(2)}, u32[]{:S(2)}) collective-permute-start(f32[192]{0:T(256)S(1)} %bitcast.230), channel_id=1, source_target_pairs={{0,4},{4,8},{8,12},{12,0},{1,5},{5,9},{9,13},{13,1},{2,6},{6,10},{... | collective-permute-start | bytes 2312 | tf_op jit(solution)/shard_map/ppermute | solution.py:10
  439.9 3.3 copy-start.1
  445.2 1.4 copy-start.2
  586.2 79.1 %copy-start.7 = (f32[768,385]{0,1:T(8,128)S(1)}, f32[768,385]{0,1:T(8,128)}, u32[]{:S(2)}) copy-start(f32[768,385]{0,1:T(8,128)} %pad_maximum_fusion.1) | copy-start | bytes 3548164
  675.6 37.2 %all-gather.15.cloned.1.call-start = ((), (), s32[]{:S(2)}) async-start(), calls=%async_computation.8 | async-start | bytes 1474560 | tf_op jit(solution)/shard_map/all_gather | solution.py:46
  676.9 42.0 %collective-permute-start.11 = (f32[192]{0:T(256)S(1)}, f32[192]{0:T(256)S(1)}, u32[]{:S(2)}, u32[]{:S(2)}) collective-permute-start(f32[192]{0:T(256)S(1)} %bitcast.227), channel_id=1, source_target_pairs={{0,8},{4,12},{8,0},{12,4},{1,9},{5,13},{9,1},{13,5},{2,10},{6,14},... | collective-permute-start | bytes 2312 | tf_op jit(solution)/shard_map/ppermute | solution.py:10
  693.1 57.9 %copy-start.9 = (bf16[768,768]{1,0:T(8,128)(2,1)S(1)}, bf16[768,768]{1,0:T(8,128)(2,1)}, u32[]{:S(2)}) copy-start(bf16[768,768]{1,0:T(8,128)(2,1)} %all-gather.17.cloned.1.call-done) | copy-start | bytes 3538948
  695.9 56.6 %collective-permute-start.9 = (f32[192,768]{1,0:T(8,128)}, f32[192,768]{1,0:T(8,128)}, u32[]{:S(2)}, u32[]{:S(2)}) collective-permute-start(f32[192,768]{1,0:T(8,128)} %fusion.107), channel_id=1, source_target_pairs={{0,8},{4,12},{8,0},{12,4},{1,9},{5,13},{9,1},{13,5},{2,10},{6,14},... | collective-permute-start | bytes 1769480 | tf_op jit(solution)/shard_map/ppermute | solution.py:10
  715.4 37.1 %copy-start.4 = (f32[192,768]{1,0:T(8,128)S(1)}, f32[192,768]{1,0:T(8,128)}, u32[]{:S(2)}) copy-start(f32[192,768]{1,0:T(8,128)} %subtract_select_fusion) | copy-start | bytes 1769476
  715.4 37.1 %collective-permute-start.8 = (f32[192,768]{1,0:T(8,128)}, f32[192,768]{1,0:T(8,128)}, u32[]{:S(2)}, u32[]{:S(2)}) collective-permute-start(f32[192,768]{1,0:T(8,128)} %fusion.153), channel_id=1, source_target_pairs={{0,8},{4,12},{8,0},{12,4},{1,9},{5,13},{9,1},{13,5},{2,10},{6,14},... | collective-permute-start | bytes 1769480 | tf_op jit(solution)/shard_map/ppermute | solution.py:10
  718.3 32.2 %collective-permute-start.10 = (f32[192]{0:T(256)S(1)}, f32[192]{0:T(256)S(1)}, u32[]{:S(2)}, u32[]{:S(2)}) collective-permute-start(f32[192]{0:T(256)S(1)} %bitcast.228), channel_id=1, source_target_pairs={{0,8},{4,12},{8,0},{12,4},{1,9},{5,13},{9,1},{13,5},{2,10},{6,14},... | collective-permute-start | bytes 2312 | tf_op jit(solution)/shard_map/ppermute | solution.py:10
Sparse Core Ops, SparseCore 0:
  50.7 31.9 reduce-scatter.3
  84.9 24.1 all-gather.6
  346.9 15.3 all-gather.8
  363.7 17.4 all-gather.10
  403.7 22.2 all-gather.12
  675.7 17.3 all-gather.16
  695.3 17.4 all-gather.14
where the time goes:
time: 770 us; the launch traced here: 762 us
  other arithmetic  389 us (51%)
  waiting for transfers between devices  179 us (23%)
  matrix products  62.4 us (8%)
  local copies, waits for them, and re-layouts  53.5 us (7%)
  starting transfers between devices  33.7 us (4%)
  between operations  25.9 us (3%)
  blocking collectives  18.3 us (2%)
    another operation x45, other arithmetic, eliminate(): factor = jnp.linalg.cholesky(full_diag)  248 us
    another operation x5, other arithmetic, eliminate(): lax.linalg.triangular_solve(factor, stacked, left_side=True, lower=True)  121 us
    ppermute x12, waiting for transfers between devices, from_behind(): return lax.ppermute(value, axis, pairs)  80.5 us
    all_gather x4, waiting for transfers between devices, eliminate(): lax.all_gather((left_rows, right_rows), ('space', 'obs'), axis=0, tiled=T...  56.8 us
    another operation x39, local copies, waits for them, and re-layouts, eliminate(): lax.linalg.triangular_solve(factor, stacked, left_side=True, lower=True)  34.1 us
    another operation x22, matrix products, eliminate(): lax.linalg.triangular_solve(factor, stacked, left_side=True, lower=True)  24 us
    another operation x20, matrix products, eliminate(): factor = jnp.linalg.cholesky(full_diag)  19.6 us
    all_to_all x1, waiting for transfers between devices, local(): lax.all_to_all(send_design.reshape(n_times, capacity, node_count), 'tm',...  19.2 us
  transfers between devices with their start and end apart: 22, of which 13 were waited for; matrix products, arithmetic and copies ran while one was open for 4% of the time, Pallas kernels for 0%

commit v1 on v0

--- a/solution.py
+++ b/solution.py
@@ -1,6 +1,8 @@
 import jax
 import jax.numpy as jnp
 from jax import lax
+from jax.experimental import pallas as pl
+from jax.experimental.pallas import tpu as pltpu
 from jax.sharding import PartitionSpec as P
 
 
@@ -17,14 +19,174 @@
     return route_time * capacity + rank
 
 
-def row_products(left_rows, right_rows):
-    return lax.dot_general(
-        left_rows, right_rows, (((1,), (1,)), ((), ())), preferred_element_type=jnp.float32
-    )
-
-
 def to_time(payload, shift_by):
     return from_behind(payload, "tm", shift_by)
+
+
+BLOCK = 128
+PANEL = 8
+HIGHEST = lax.Precision.HIGHEST
+
+
+def across(value, lane_index):
+    return jnp.broadcast_to(value[:, lane_index : lane_index + 1], value.shape)
+
+
+def down(value, row_index):
+    return jnp.broadcast_to(value[row_index : row_index + 1, :], value.shape)
+
+
+def tree_sum(terms):
+    terms = list(terms)
+    while len(terms) > 1:
+        terms = [
+            terms[at] + terms[at + 1] if at + 1 < len(terms) else terms[at]
+            for at in range(0, len(terms), 2)
+        ]
+    return terms[0]
+
+
+def dot32(left, right, dims=((1,), (0,))):
+    return lax.dot_general(
+        left, right, (dims, ((), ())), precision=HIGHEST, preferred_element_type=jnp.float32
+    )
+
+
+def halves(value):
+    high = value.astype(jnp.bfloat16)
+    return high, (value - high.astype(jnp.float32)).astype(jnp.bfloat16)
+
+
+def dot_halves(left, right, dims=((1,), (0,))):
+    def one(a, b):
+        return lax.dot_general(a, b, (dims, ((), ())), preferred_element_type=jnp.float32)
+
+    return one(left[0], right[0]) + (one(left[0], right[1]) + one(left[1], right[0]))
+
+
+def panel_step(panel, first, lane, sub, ones):
+    cols = [across(panel, first + j) * ones for j in range(PANEL)]
+    entry = [[None] * PANEL for _ in range(PANEL)]
+    for i in range(PANEL):
+        for j in range(i, PANEL):
+            entry[i][j] = entry[j][i] = down(cols[j], i)
+    inside = (lane >= first) & (lane < first + PANEL)
+    augmented = jnp.where(inside, jnp.where(lane == first + sub, 1.0, 0.0), panel)
+    lower = jnp.where(lane < first + PANEL, augmented, 0.0)
+    rows = [down(augmented, i) for i in range(PANEL)]
+    for j in range(0, PANEL, 2):
+        p, b, s = entry[j][j], entry[j][j + 1], entry[j + 1][j + 1]
+        r = 1.0 / (p * s - b * b)
+        upper_new, lower_new = {}, {}
+        for m in range(j + 2, PANEL):
+            upper_new[m] = (s * entry[j][m] - b * entry[j + 1][m]) * r
+            lower_new[m] = (p * entry[j + 1][m] - b * entry[j][m]) * r
+        upper_row = (s * rows[j] - b * rows[j + 1]) * r
+        lower_row = (p * rows[j + 1] - b * rows[j]) * r
+        for i in range(PANEL):
+            if i in (j, j + 1):
+                continue
+            f, g = entry[i][j], entry[i][j + 1]
+            for m in range(max(j + 2, i if i > j else 0), PANEL):
+                value = entry[i][m] - (f * upper_new[m] + g * lower_new[m])
+                entry[i][m] = value
+                if i > j and m > i:
+                    entry[m][i] = value
+            rows[i] = rows[i] - (f * upper_row + g * lower_row)
+        for m in range(j + 2, PANEL):
+            entry[j][m] = upper_new[m]
+            entry[j + 1][m] = lower_new[m]
+        rows[j], rows[j + 1] = upper_row, lower_row
+    solved = rows[0]
+    for i in range(1, PANEL):
+        solved = jnp.where(sub == i, rows[i], solved)
+    return lower, rows, solved, inside
+
+
+def factor_block(block, lower_ref, scaled_ref, ones):
+    count = BLOCK // PANEL
+    lane = lax.broadcasted_iota(jnp.int32, (PANEL, BLOCK), 1)
+    sub = lax.broadcasted_iota(jnp.int32, (PANEL, BLOCK), 0)
+    rows = [block[PANEL * i : PANEL * (i + 1), :] for i in range(count)]
+    for q in range(count):
+        first = q * PANEL
+        lower, pivot_rows, solved, inside = panel_step(rows[q], first, lane, sub, ones)
+        lower_ref[first : first + PANEL, :] = lower
+        scaled_ref[first : first + PANEL, :] = jnp.where(lane < first + PANEL, solved, 0.0)
+        for i in range(q + 1, count):
+            change = tree_sum(
+                across(rows[i], first + j) * pivot_rows[j] for j in range(PANEL)
+            )
+            rows[i] = jnp.where(inside, 0.0, rows[i]) - change
+
+
+def solve_kernel(diag_ref, cols_ref, out_ref, work_ref, lower_ref, scaled_ref, ones_ref):
+    blocks = diag_ref.shape[0] // BLOCK
+    ones_ref[...] = jnp.ones_like(ones_ref)
+    ones = ones_ref[...]
+    work_ref[...] = diag_ref[...]
+    out_ref[...] = cols_ref[...]
+    current = diag_ref[0:BLOCK, 0:BLOCK]
+    for p in range(blocks):
+        at, after = p * BLOCK, (p + 1) * BLOCK
+        last = p == blocks - 1
+        slot = p % 2
+        factor_block(current, lower_ref.at[slot], scaled_ref.at[slot], ones)
+        lower, scaled = lower_ref[slot], scaled_ref[slot]
+        if not last:
+            below = dot32(work_ref[after : after + BLOCK, at:after], lower, ((1,), (1,)))
+            beside = dot32(scaled, work_ref[at:after, after : after + BLOCK])
+            current = work_ref[after : after + BLOCK, after : after + BLOCK] - dot32(below, beside)
+        inverse = halves(dot32(lower, scaled, ((0,), (0,))))
+        if not last:
+            panel = dot_halves(inverse, halves(work_ref[at:after, after:]))
+            panel_parts = halves(panel)
+        panel_cols = dot_halves(inverse, halves(out_ref[at:after, :]))
+        panel_cols_parts = halves(panel_cols)
+        for i in range(blocks):
+            if i == p:
+                continue
+            rows = slice(i * BLOCK, (i + 1) * BLOCK)
+            column = halves(work_ref[rows, at:after])
+            if not last:
+                work_ref[rows, after:] -= dot_halves(column, panel_parts)
+            out_ref[rows, :] -= dot_halves(column, panel_cols_parts)
+        if not last:
+            work_ref[at:after, after:] = panel
+        out_ref[at:after, :] = panel_cols
+
+
+def solve(diag, cols):
+    nodes, width = cols.shape
+    assert nodes % BLOCK == 0, nodes
+    whole = pl.BlockSpec(memory_space=pltpu.VMEM)
+    return pl.pallas_call(
+        solve_kernel,
+        out_shape=jax.ShapeDtypeStruct((nodes, width), jnp.float32),
+        in_specs=[whole, whole],
+        out_specs=whole,
+        scratch_shapes=[
+            pltpu.VMEM((nodes, nodes), jnp.float32),
+            pltpu.VMEM((2, BLOCK, BLOCK), jnp.float32),
+            pltpu.VMEM((2, BLOCK, BLOCK), jnp.float32),
+            pltpu.VMEM((PANEL, BLOCK), jnp.float32),
+        ],
+        cost_estimate=pl.CostEstimate(
+            flops=40 * nodes * nodes * nodes, bytes_accessed=4 * nodes * nodes, transcendentals=0
+        ),
+        name="solve_spd",
+    )(diag, cols)
+
+
+def product(columns, full_rows):
+    high, low = halves(columns)
+
+    def one(part):
+        return lax.dot_general(
+            part, full_rows, (((0,), (1,)), ((), ())), preferred_element_type=jnp.float32
+        )
+
+    return one(high) + one(low)
 
 
 def eliminate(diag_rows, rhs_rows, left_cols, right_cols, with_turn):
@@ -33,30 +195,28 @@
         lax.all_gather(diag_rows, ("space", "obs"), axis=0, tiled=True),
         lax.all_gather(rhs_rows, ("space", "obs"), axis=0, tiled=True),
     )
-    factor = jnp.linalg.cholesky(full_diag)
-    stacked = jnp.concatenate([left_cols, right_cols, full_rhs[:, None]], axis=1)
-    solved = lax.linalg.triangular_solve(factor, stacked, left_side=True, lower=True)
-    left_y = solved[:, :shard_rows]
-    right_y = solved[:, shard_rows : 2 * shard_rows]
-    reduced = solved[:, 2 * shard_rows]
-    up_left = jnp.dot(reduced, left_y, precision=lax.Precision.HIGHEST)
-    up_right = jnp.dot(reduced, right_y, precision=lax.Precision.HIGHEST)
-    left_rows = left_y.T.astype(jnp.bfloat16)
-    right_rows = right_y.T.astype(jnp.bfloat16)
-    piece_left, piece_right = lax.all_gather(
-        (left_rows, right_rows), ("space", "obs"), axis=0, tiled=True
-    )
-    results = (
-        row_products(left_rows, piece_left),
-        row_products(right_rows, piece_right),
-        -row_products(left_rows, piece_right),
-    )
-    if with_turn:
-        results = results + (-row_products(right_rows, piece_left),)
+    left_full, right_full = lax.all_gather(
+        (left_cols.T.astype(jnp.bfloat16), right_cols.T.astype(jnp.bfloat16)),
+        ("space", "obs"),
+        axis=0,
+        tiled=True,
+    )
+    solved = solve(full_diag, jnp.concatenate([left_cols, right_cols], axis=1))
+    left_x = solved[:, :shard_rows]
+    right_x = solved[:, shard_rows:]
+    up_left = jnp.dot(full_rhs, left_x, precision=HIGHEST)
+    up_right = jnp.dot(full_rhs, right_x, precision=HIGHEST)
     turned = None
     if with_turn:
-        turned = results[3]
-    return (results[0], results[1], results[2], turned, up_left, up_right)
+        turned = -product(right_x, left_full)
+    return (
+        product(left_x, left_full),
+        product(right_x, right_full),
+        -product(left_x, right_full),
+        turned,
+        up_left,
+        up_right,
+    )
 
 
 def local(obs_panel, node_index, weight, residual, route_time, spatial_prec, ar_coef, prior_rhs):

time: 770 us -> 341 us (0.44)
  other arithmetic: 389 us -> 16.2 us
  Pallas kernels: 0 us -> 47.5 us
  local copies, waits for them, and re-layouts: 53.5 us -> 11.6 us
  matrix products: 62.4 us -> 25.1 us
  waiting for transfers between devices: 179 us -> 167 us
  between operations: 25.9 us -> 18 us
    another operation x52 -> x2, other arithmetic: 370 us -> 1.24 us  [the longest x45 248 us: eliminate(): factor = jnp.linalg.cholesky(full_diag)]
    all_gather x4, waiting for transfers between devices: 56.8 us -> 7.74 us  [eliminate(): lax.all_gather((left_cols.T.astype(jnp.bfloat16), right_cols.T.astype(jnp...]
    pallas_call x0 -> x2, Pallas kernels: none -> 47.5 us  [solve(): pl.pallas_call(solve_kernel, out_shape=jax.ShapeDtypeStruct((nodes, width...]
    another operation x42 -> x0, matrix products: 43.6 us -> none  [the longest x22 24 us: eliminate(): lax.linalg.triangular_solve(factor, stacked, left_side=True, lower=True)]
    another operation x55 -> x2, local copies, waits for them, and re-layouts: 34.7 us -> 0.1 us  [the longest x39 34.1 us: eliminate(): lax.linalg.triangular_solve(factor, stacked, left_side=True, lower=True)]
    all_gather x2, waiting for transfers between devices: 0.01 us -> 21.7 us  [eliminate(): lax.all_gather(diag_rows, ('space', 'obs'), axis=0, tiled=True)]
    ppermute x12, waiting for transfers between devices: 80.5 us -> 96.8 us  [from_behind(): return lax.ppermute(value, axis, pairs)]
    dot_general x11 -> x18, matrix products: 16.2 us -> 22.5 us  [the longest x14 18.2 us: one(): lax.dot_general(part, full_rows, (((0,), (1,)), ((), ())), preferred_elem...]
  transfers between devices with their start and end apart: 22 -> 22, of which waited for: 13 -> 14; matrix products, arithmetic and copies ran while one was open for 4% -> 11% of each run, Pallas kernels for 0% -> 14%
where the time goes in v1:
time: 341 us; the launch traced here: 336 us
  waiting for transfers between devices  167 us (49%)
  Pallas kernels  47.5 us (14%)
  starting transfers between devices  32.6 us (10%)
  matrix products  25.1 us (7%)
  blocking collectives  18.1 us (5%)
  between operations  18 us (5%)
  other arithmetic  16.2 us (5%)
  local copies, waits for them, and re-layouts  11.6 us (3%)
    ppermute x12, waiting for transfers between devices, from_behind(): return lax.ppermute(value, axis, pairs)  96.8 us
    pallas_call x2, Pallas kernels, solve(): pl.pallas_call(solve_kernel, out_shape=jax.ShapeDtypeStruct((nodes, width...  47.5 us
    all_gather x2, waiting for transfers between devices, eliminate(): lax.all_gather(diag_rows, ('space', 'obs'), axis=0, tiled=True)  21.7 us
    all_to_all x1, waiting for transfers between devices, local(): lax.all_to_all(send_design.reshape(n_times, capacity, node_count), 'tm',...  19.2 us
    dot_general x14, matrix products, one(): lax.dot_general(part, full_rows, (((0,), (1,)), ((), ())), preferred_elem...  18.2 us
    ppermute x12, starting transfers between devices, from_behind(): return lax.ppermute(value, axis, pairs)  17.7 us
    reduce_scatter x1, waiting for transfers between devices, local(): lax.psum_scatter(lax.dot_general(slot_design, weighted, (((0,), (0,)), ((...  14.5 us
    unnamed x2, blocking collectives  11.6 us
  transfers between devices with their start and end apart: 22, of which 14 were waited for; matrix products, arithmetic and copies ran while one was open for 11% of the time, Pallas kernels for 14%

profile of v1, /device:TPU:0, one launch (start us, length us, event | category | flops | bytes accessed | tf_op | source)
XLA Modules:
  0.0 336.0 jit_solution(15371709405910184063)
XLA Ops:
  7.8 1.2 reduce-window.6
  10.8 2.3 scatter_custom_fusion.1
  13.7 6.3 %all-to-all-start.1 = ((bf16[4,1,128]{2,1,0:T(2,128)(2,1)}), bf16[4,1,128]{2,1,0:T(2,128)(2,1)S(1)}, u32[]{:S(2)}, u32[]{:S(2)}) async-start(bf16[4,1,128]{2,1,0:T(2,128)(2,1)} %copy.45), calls=%async_computation.1 | async-start | bytes 4096 | tf_op jit(solution)/shard_map/all_to_all | solution.py:247
  20.1 2.5 scatter_custom_fusion
  23.7 1.8 all-to-all-done.1
  25.6 3.5 %all-to-all-start = ((bf16[4,128,768]{1,2,0:T(8,128)(2,1)}), bf16[4,128,768]{1,2,0:T(8,128)(2,1)S(1)}, u32[]{:S(2)}, u32[]{:S(2)}) async-start(bf16[4,128,768]{1,2,0:T(8,128)(2,1)} %copy.44), calls=%async_computation | async-start | bytes 1572864 | tf_op jit(solution)/shard_map/all_to_all | solution.py:240
  29.1 19.2 %all-to-all-done = bf16[4,128,768]{1,2,0:T(8,128)(2,1)S(1)} async-done(((bf16[4,128,768]{1,2,0:T(8,128)(2,1)}), bf16[4,128,768]{1,2,0:T(8,128)(2,1)S(1)}, u32[]{:S(2)}, u32[]{:S(2)}) %all-to-all-start) | async-done | bytes 786464 | tf_op jit(solution)/shard_map/all_to_all | solution.py:240
  48.4 2.3 convolution_bitcast_fusion
  51.7 1.5 collective-permute-start.1
  53.9 12.2 %collective-permute-done = f32[1]{0:T(128)} collective-permute-done((f32[1]{0:T(128)}, f32[1]{0:T(128)}, u32[]{:S(2)}, u32[]{:S(2)}) %collective-permute-start) | collective-permute-done | bytes 36 | tf_op jit(solution)/shard_map/ppermute | solution.py:12
  68.2 14.5 %reduce-scatter.2.cloned.1.call-done = f32[192,768]{1,0:T(8,128)} async-done(((f32[768,768]{1,0:T(8,128)}), f32[192,768]{1,0:T(8,128)}) %reduce-scatter.2.cloned.1.call-update) | async-done | bytes 589840 | tf_op jit(solution)/shard_map/reduce_scatter | solution.py:261
  82.7 2.2 multiply_convert_fusion.3
  85.8 1.4 copy.47.cols_ref
  87.5 21.7 %all-gather.7.cloned.1.call-done.diag_ref = f32[768,768]{1,0:T(8,128)} async-done(((f32[192,768]{1,0:T(8,128)}), f32[768,768]{1,0:T(8,128)}) %all-gather.7.cloned.1.call-update) | async-done | bytes 2359312 | tf_op jit(solution)/shard_map/all_gather | solution.py:195
  109.1 23.8 %solve_spd.2 = f32[768,384]{1,0:T(8,128)} custom-call(f32[768,768]{1,0:T(8,128)} %all-gather.7.cloned.1.call-done.diag_ref, f32[768,384]{1,0:T(8,128)} %copy.47.cols_ref), custom_call_target="tpu_custom_call" | custom-call | flops 18119393280 | bytes 2359296 | tf_op jit(solution)/shard_map/solve_spd/pallas_call | solution.py:163
  132.9 2.2 fusion.28
  135.2 1.4 convolution_add_fusion.6
  136.6 3.3 collective-permute-start.2
  139.9 7.7 %all-gather.11.cloned.1.call-done = bf16[768,768]{1,0:T(8,128)(2,1)} async-done(((bf16[192,768]{1,0:T(8,128)(2,1)}), bf16[768,768]{1,0:T(8,128)(2,1)}) %all-gather.11.cloned.1.call-update) | async-done | bytes 1179664 | tf_op jit(solution)/shard_map/all_gather | solution.py:198
  147.6 2.2 fusion.31
  149.8 1.5 convolution_add_fusion.5
  151.4 1.5 collective-permute-start.3
  153.2 15.8 %collective-permute-done.3 = f32[192,768]{1,0:T(8,128)} collective-permute-done((f32[192,768]{1,0:T(8,128)}, f32[192,768]{1,0:T(8,128)}, u32[]{:S(2)}, u32[]{:S(2)}) %collective-permute-start.3) | collective-permute-done | bytes 589856 | tf_op jit(solution)/shard_map/ppermute | solution.py:12
  168.9 2.3 subtract_select_fusion
  173.0 1.6 collective-permute-start.5
  174.5 13.1 %collective-permute-done.5 = f32[192,768]{1,0:T(8,128)S(1)} collective-permute-done((f32[192,768]{1,0:T(8,128)S(1)}, f32[192,768]{1,0:T(8,128)S(1)}, u32[]{:S(2)}, u32[]{:S(2)}) %collective-permute-start.5) | collective-permute-done | bytes 589856 | tf_op jit(solution)/shard_map/ppermute | solution.py:12
  189.3 2.2 scatter_custom_fusion.2
  192.0 4.6 %all-to-all-start.2 = ((bf16[4,1,128]{2,1,0:T(2,128)(2,1)}), bf16[4,1,128]{2,1,0:T(2,128)(2,1)S(1)}, u32[]{:S(2)}, u32[]{:S(2)}) async-start(bf16[4,1,128]{2,1,0:T(2,128)(2,1)} %copy.50), calls=%async_computation.3 | async-start | bytes 4096 | tf_op jit(solution)/shard_map/all_to_all | solution.py:250
  197.8 4.3 %all-to-all-done.2 = bf16[4,1,128]{2,1,0:T(2,128)(2,1)S(1)} async-done(((bf16[4,1,128]{2,1,0:T(2,128)(2,1)}), bf16[4,1,128]{2,1,0:T(2,128)(2,1)S(1)}, u32[]{:S(2)}, u32[]{:S(2)}) %all-to-all-start.2) | async-done | bytes 1056 | tf_op jit(solution)/shard_map/all_to_all | solution.py:250
  202.5 6.5 %psum.7 = f32[768]{0:T(1024)S(1)} all-reduce(f32[768]{0:T(1024)S(1)} %convolution_reduce_fusion), channel_id=1, replica_groups=mesh['grp'=2,'tm'=4,'space'=2,'obs'=2] {'space','obs'}, use_global_device_ids=true, to_apply=%region_7.8 | all-reduce | flops 768 | bytes 6144 | tf_op jit(solution)/shard_map/psum | solution.py:269
  209.2 5.7 %all-reduce = f32[768]{0:T(1024)S(1)} all-reduce(f32[768]{0:T(1024)S(1)} %fusion.27), channel_id=1, replica_groups=mesh['grp'=2,'tm'=4,'space'=2,'obs'=2] {'space','obs'}, use_global_device_ids=true, to_apply=%add | all-reduce | flops 768 | bytes 6144
  216.9 3.5 %collective-permute-start.8 = (f32[192]{0:T(256)S(1)}, f32[192]{0:T(256)S(1)}, u32[]{:S(2)}, u32[]{:S(2)}) collective-permute-start(f32[192]{0:T(256)S(1)} %bitcast.87), channel_id=1, source_target_pairs={{0,12},{4,0},{8,4},{12,8},{1,13},{5,1},{9,5},{13,9},{2,14},{6,2},{... | collective-permute-start | bytes 2312 | tf_op jit(solution)/shard_map/ppermute | solution.py:12
  221.0 8.1 %collective-permute-done.8 = f32[192]{0:T(256)S(1)} collective-permute-done((f32[192]{0:T(256)S(1)}, f32[192]{0:T(256)S(1)}, u32[]{:S(2)}, u32[]{:S(2)}) %collective-permute-start.8) | collective-permute-done | bytes 800 | tf_op jit(solution)/shard_map/ppermute | solution.py:12
  229.1 3.9 %collective-permute-done.9 = f32[192]{0:T(256)S(1)} collective-permute-done((f32[192]{0:T(256)S(1)}, f32[192]{0:T(256)S(1)}, u32[]{:S(2)}, u32[]{:S(2)}) %collective-permute-start.9) | collective-permute-done | bytes 800 | tf_op jit(solution)/shard_map/ppermute | solution.py:12
  233.2 5.9 %all-reduce.1 = f32[768]{0:T(1024)S(1)} all-reduce(f32[768]{0:T(1024)S(1)} %get-tuple-element.9), channel_id=1, replica_groups=mesh['grp'=2,'tm'=4,'space'=2,'obs'=2] {'space','obs'}, use_global_device_ids=true, to_apply=%add.1 | all-reduce | flops 768 | bytes 6144
  240.5 1.3 pad_maximum_fusion.1.cols_ref
  241.8 23.7 %solve_spd.3 = f32[768,384]{1,0:T(8,128)} custom-call(f32[768,768]{1,0:T(8,128)} %all-gather.13.cloned.1.call-done.diag_ref, f32[768,384]{1,0:T(8,128)} %pad_maximum_fusion.1.cols_ref), custom_call_target="tpu_custom_call" | custom-call | flops 18119393280 | bytes 2359296 | tf_op jit(solution)/shard_map/solve_spd/pallas_call | solution.py:163
  265.5 1.6 fusion.9
  267.6 1.7 fusion.7
  269.3 2.5 collective-permute-start.11
  271.8 2.2 fusion.16
  274.0 1.6 convolution_add_fusion.1
  276.0 1.9 fusion.33
  278.5 2.6 collective-permute-start.6
  281.7 1.4 fusion.5
  283.6 30.9 %collective-permute-done.7 = f32[192,768]{1,0:T(8,128)} collective-permute-done((f32[192,768]{1,0:T(8,128)}, f32[192,768]{1,0:T(8,128)}, u32[]{:S(2)}, u32[]{:S(2)}) %collective-permute-start.7) | collective-permute-done | bytes 589856 | tf_op jit(solution)/shard_map/ppermute | solution.py:12
  314.5 12.4 %collective-permute-done.6 = f32[192,768]{1,0:T(8,128)S(1)} collective-permute-done((f32[192,768]{1,0:T(8,128)S(1)}, f32[192,768]{1,0:T(8,128)S(1)}, u32[]{:S(2)}, u32[]{:S(2)}) %collective-permute-start.6) | collective-permute-done | bytes 589856 | tf_op jit(solution)/shard_map/ppermute | solution.py:12
  327.0 2.0 select_bitcast_fusion
  (96 shorter events, 18.3 us)
Async XLA Ops:
  13.7 11.8 %all-to-all-start.1 = ((bf16[4,1,128]{2,1,0:T(2,128)(2,1)}), bf16[4,1,128]{2,1,0:T(2,128)(2,1)S(1)}, u32[]{:S(2)}, u32[]{:S(2)}) async-start(bf16[4,1,128]{2,1,0:T(2,128)(2,1)} %copy.45), calls=%async_computation.1 | async-start | bytes 4096 | tf_op jit(solution)/shard_map/all_to_all | solution.py:247
  25.6 22.8 %all-to-all-start = ((bf16[4,128,768]{1,2,0:T(8,128)(2,1)}), bf16[4,128,768]{1,2,0:T(8,128)(2,1)S(1)}, u32[]{:S(2)}, u32[]{:S(2)}) async-start(bf16[4,128,768]{1,2,0:T(8,128)(2,1)} %copy.44), calls=%async_computation | async-start | bytes 1572864 | tf_op jit(solution)/shard_map/all_to_all | solution.py:240
  29.1 53.6 %reduce-scatter.2.cloned.1.call-start = ((), (), s32[]{:S(2)}) async-start(), calls=%async_computation.4 | async-start | bytes 2949120 | tf_op jit(solution)/shard_map/reduce_scatter | solution.py:261
  48.4 2.3 copy-start.5
  50.6 1.1 copy-start.11
  50.6 58.5 %all-gather.7.cloned.1.call-start = ((), (), s32[]{:S(2)}) async-start(), calls=%async_computation.5 | async-start | bytes 2949120 | tf_op jit(solution)/shard_map/all_gather | solution.py:195
  51.7 16.5 %collective-permute-start.1 = (f32[192,768]{1,0:T(8,128)S(1)}, f32[192,768]{1,0:T(8,128)S(1)}, u32[]{:S(2)}, u32[]{:S(2)}) collective-permute-start(f32[192,768]{1,0:T(8,128)S(1)} %bitcast.79), channel_id=1, source_target_pairs={{0,12},{4,0},{8,4},{12,8},{1,13},{5,1},{9,5},{13,9},{2,14},{6,2},{... | collective-permute-start | bytes 1769480 | tf_op jit(solution)/shard_map/ppermute | solution.py:12
  53.2 12.9 %collective-permute-start = (f32[1]{0:T(128)}, f32[1]{0:T(128)}, u32[]{:S(2)}, u32[]{:S(2)}) collective-permute-start(f32[1]{0:T(128)} %param.14), channel_id=1, source_target_pairs={{0,12},{4,0},{8,4},{12,8},{1,13},{5,1},{9,5},{13,9},{2,14},{6,2},{... | collective-permute-start | bytes 20 | tf_op jit(solution)/shard_map/ppermute | solution.py:12
  84.9 48.0 %all-gather.9.cloned.1.call-start = ((), (), s32[]{:S(2)}) async-start(), calls=%async_computation.6 | async-start | bytes 1474560 | tf_op jit(solution)/shard_map/all_gather | solution.py:198
  85.7 62.0 %all-gather.11.cloned.1.call-start = ((), (), s32[]{:S(2)}) async-start(), calls=%async_computation.7 | async-start | bytes 1474560 | tf_op jit(solution)/shard_map/all_gather | solution.py:198
  87.2 154.6 %all-gather.13.cloned.1.call-start = ((), (), s32[]{:S(2)}) async-start(), calls=%async_computation.8 | async-start | bytes 2949120 | tf_op jit(solution)/shard_map/all_gather | solution.py:195
  132.9 2.2 copy-start
  132.9 2.2 copy-start.3
  136.6 16.6 %collective-permute-start.2 = (f32[192,768]{1,0:T(8,128)}, f32[192,768]{1,0:T(8,128)}, u32[]{:S(2)}, u32[]{:S(2)}) collective-permute-start(f32[192,768]{1,0:T(8,128)} %convolution_add_fusion.6), channel_id=1, source_target_pairs={{0,12},{4,0},{8,4},{12,8},{1,13},{5,1},{9,5},{13,9},{2,14},{6,2},{... | collective-permute-start | bytes 1769480 | tf_op jit(solution)/shard_map/ppermute | solution.py:12
  147.6 2.2 copy-start.2
  151.4 17.6 %collective-permute-start.3 = (f32[192,768]{1,0:T(8,128)}, f32[192,768]{1,0:T(8,128)}, u32[]{:S(2)}, u32[]{:S(2)}) collective-permute-start(f32[192,768]{1,0:T(8,128)} %convolution_add_fusion.5), channel_id=1, source_target_pairs={{0,4},{4,8},{8,12},{12,0},{1,5},{5,9},{9,13},{13,1},{2,6},{6,10},{... | collective-permute-start | bytes 1769480 | tf_op jit(solution)/shard_map/ppermute | solution.py:12
  171.3 100.5 %all-gather.17.cloned.1.call-start = ((), (), s32[]{:S(2)}) async-start(), calls=%async_computation.10 | async-start | bytes 1474560 | tf_op jit(solution)/shard_map/all_gather | solution.py:198
  172.9 16.3 %copy-start.13 = (bf16[256]{0:T(256)(128)(2,1)S(1)}, bf16[256]{0:T(256)(128)(2,1)}, u32[]{:S(2)}) copy-start(bf16[256]{0:T(256)(128)(2,1)} %param.10) | copy-start | bytes 1540
  172.9 16.3 %copy-start.14 = (bf16[256]{0:T(256)(128)(2,1)S(1)}, bf16[256]{0:T(256)(128)(2,1)}, u32[]{:S(2)}) copy-start(bf16[256]{0:T(256)(128)(2,1)} %param.11) | copy-start | bytes 1540
  172.9 23.7 %copy-start.15 = (u32[32]{0:T(128)S(1)}, u32[32]{0:T(128)}, u32[]{:S(2)}) copy-start(u32[32]{0:T(128)} %constant.63) | copy-start | bytes 388
  172.9 29.2 %copy-start.6 = (bf16[4,128,768]{1,2,0:T(8,128)(2,1)S(1)}, bf16[4,128,768]{1,2,0:T(8,128)(2,1)}, u32[]{:S(2)}) copy-start(bf16[4,128,768]{1,2,0:T(8,128)(2,1)} %copy-done.5) | copy-start | bytes 2359300
  172.9 36.1 %copy-start.12 = (f32[1,192]{1,0:T(1,128)S(1)}, f32[1,192]{1,0:T(1,128)}, u32[]{:S(2)}) copy-start(f32[1,192]{1,0:T(1,128)} %param.15) | copy-start | bytes 2308
  173.0 14.7 %collective-permute-start.5 = (f32[192,768]{1,0:T(8,128)S(1)}, f32[192,768]{1,0:T(8,128)S(1)}, u32[]{:S(2)}, u32[]{:S(2)}) collective-permute-start(f32[192,768]{1,0:T(8,128)S(1)} %fusion.1), channel_id=1, source_target_pairs={{0,12},{4,0},{8,4},{12,8},{1,13},{5,1},{9,5},{13,9},{2,14},{6,2},{... | collective-permute-start | bytes 1769480 | tf_op jit(solution)/shard_map/ppermute | solution.py:12
  187.6 0.8 copy-start.9
  192.0 10.2 %all-to-all-start.2 = ((bf16[4,1,128]{2,1,0:T(2,128)(2,1)}), bf16[4,1,128]{2,1,0:T(2,128)(2,1)S(1)}, u32[]{:S(2)}, u32[]{:S(2)}) async-start(bf16[4,1,128]{2,1,0:T(2,128)(2,1)} %copy.50), calls=%async_computation.3 | async-start | bytes 4096 | tf_op jit(solution)/shard_map/all_to_all | solution.py:250
  196.6 79.4 %all-gather.15.cloned.1.call-start = ((), (), s32[]{:S(2)}) async-start(), calls=%async_computation.9 | async-start | bytes 1474560 | tf_op jit(solution)/shard_map/all_gather | solution.py:198
  216.1 23.0 %collective-permute-start.4 = (f32[192,768]{1,0:T(8,128)S(1)}, f32[192,768]{1,0:T(8,128)S(1)}, u32[]{:S(2)}, u32[]{:S(2)}) collective-permute-start(f32[192,768]{1,0:T(8,128)S(1)} %fusion.2), channel_id=1, source_target_pairs={{0,4},{4,8},{8,12},{12,0},{1,5},{5,9},{9,13},{13,1},{2,6},{6,10},{... | collective-permute-start | bytes 1769480 | tf_op jit(solution)/shard_map/ppermute | solution.py:12
  216.9 12.2 %collective-permute-start.8 = (f32[192]{0:T(256)S(1)}, f32[192]{0:T(256)S(1)}, u32[]{:S(2)}, u32[]{:S(2)}) collective-permute-start(f32[192]{0:T(256)S(1)} %bitcast.87), channel_id=1, source_target_pairs={{0,12},{4,0},{8,4},{12,8},{1,13},{5,1},{9,5},{13,9},{2,14},{6,2},{... | collective-permute-start | bytes 2312 | tf_op jit(solution)/shard_map/ppermute | solution.py:12
  221.0 12.1 %collective-permute-start.9 = (f32[192]{0:T(256)S(1)}, f32[192]{0:T(256)S(1)}, u32[]{:S(2)}, u32[]{:S(2)}) collective-permute-start(f32[192]{0:T(256)S(1)} %bitcast.88), channel_id=1, source_target_pairs={{0,4},{4,8},{8,12},{12,0},{1,5},{5,9},{9,13},{13,1},{2,6},{6,10},{... | collective-permute-start | bytes 2312 | tf_op jit(solution)/shard_map/ppermute | solution.py:12
  239.1 1.2 copy-start.10
  265.5 6.3 %copy-start.1 = (f32[768,384]{1,0:T(8,128)S(1)}, f32[768,384]{1,0:T(8,128)}, u32[]{:S(2)}) copy-start(f32[768,384]{1,0:T(8,128)} %solve_spd.3) | copy-start | bytes 3538948
  267.2 15.9 %collective-permute-start.10 = (f32[192]{0:T(256)S(1)}, f32[192]{0:T(256)S(1)}, u32[]{:S(2)}, u32[]{:S(2)}) collective-permute-start(f32[192]{0:T(256)S(1)} %bitcast.85), channel_id=1, source_target_pairs={{0,8},{4,12},{8,0},{12,4},{1,9},{5,13},{9,1},{13,5},{2,10},{6,14},... | collective-permute-start | bytes 2312 | tf_op jit(solution)/shard_map/ppermute | solution.py:12
  269.3 13.8 %collective-permute-start.11 = (f32[192]{0:T(256)S(1)}, f32[192]{0:T(256)S(1)}, u32[]{:S(2)}, u32[]{:S(2)}) collective-permute-start(f32[192]{0:T(256)S(1)} %bitcast.86), channel_id=1, source_target_pairs={{0,8},{4,12},{8,0},{12,4},{1,9},{5,13},{9,1},{13,5},{2,10},{6,14},... | collective-permute-start | bytes 2312 | tf_op jit(solution)/shard_map/ppermute | solution.py:12
  271.8 2.2 copy-start.4
  275.6 38.9 %collective-permute-start.7 = (f32[192,768]{1,0:T(8,128)}, f32[192,768]{1,0:T(8,128)}, u32[]{:S(2)}, u32[]{:S(2)}) collective-permute-start(f32[192,768]{1,0:T(8,128)} %convolution_add_fusion.1), channel_id=1, source_target_pairs={{0,8},{4,12},{8,0},{12,4},{1,9},{5,13},{9,1},{13,5},{2,10},{6,14},... | collective-permute-start | bytes 1769480 | tf_op jit(solution)/shard_map/ppermute | solution.py:12
  276.0 1.9 copy-start.8
  278.5 48.5 %collective-permute-start.6 = (f32[192,768]{1,0:T(8,128)S(1)}, f32[192,768]{1,0:T(8,128)S(1)}, u32[]{:S(2)}, u32[]{:S(2)}) collective-permute-start(f32[192,768]{1,0:T(8,128)S(1)} %convolution_add_fusion.2), channel_id=1, source_target_pairs={{0,8},{4,12},{8,0},{12,4},{1,9},{5,13},{9,1},{13,5},{2,10},{6,14},... | collective-permute-start | bytes 1769480 | tf_op jit(solution)/shard_map/ppermute | solution.py:12
  281.6 45.3 %copy-start.7 = (f32[192,768]{1,0:T(8,128)S(1)}, f32[192,768]{1,0:T(8,128)}, u32[]{:S(2)}) copy-start(f32[192,768]{1,0:T(8,128)} %subtract_select_fusion) | copy-start | bytes 1769476
Sparse Core Ops, SparseCore 0:
  50.8 31.8 reduce-scatter.1
  85.0 24.0 all-gather.6
  111.3 17.4 all-gather.8
  130.2 17.4 all-gather.10
  171.4 22.2 all-gather.12
  195.1 17.5 all-gather.16
  240.0 14.6 all-gather.14
